TPU v7x, 512 devices: a whole 4x4x16 slice. The times are simulated.
512 devices in a mesh: row: 64 (over z_lo, y, x), col: 8 (over z_hi, core).
Axes of the slice: x: 4, y: 4, z: 16 (z_hi: 4, z_lo: 4; z = z_hi * 4 + z_lo), core: 2. Of those that a mesh axis runs over, the one named last changes fastest.
Arguments:
- front: float32 [65536, 1024], P('row', 'col'), may hold values from -6 to 6
- contrib: bfloat16 [524288, 1024], P('row', 'col'), may hold values from -6 to 6
- target: int32 [2048], replicated, may hold values from 0 to 255, as said below
- mask: int32 [256, 8], P('row', 'col'), may hold values 0 or 1
- panel: float32 [65536, 256], P(('row', 'col')), as said below
- pivots: int32 [256], replicated, may hold values from 0 to 65535, as said below
Outputs:
- lower: float32 [65536, 256], P(('row', 'col'))
- schur: float32 [65536, 1024], P('row', 'col')
Inputs may be any that keep to these rules, and one draw needn't show every extreme that they name: Front block row t lies on index t // 4 of row. Within each aligned block of 32 entries (one device's contribution blocks) the values target // 4 are distinct, and index 0 of row receives a block from every aligned block. `pivots`: distinct rows; each aligned group of 1024 rows holds exactly 4 of them. The 256 x 256 matrix formed by the panel's rows named in pivots is invertible.
All inputs are finite; a program needn't handle non-finite values. No bound on the sum of `mask` on one device may be relied on, other than what follows from the above.
Results may differ from a plain program's by a relative error of at most 0.0003.
Values may be sent and summed in bfloat16 or wider, within the bound.
No kernel may reach another device: no remote copies, remote signals or barrier semaphores. Data moves between devices by JAX's collectives and lax.ppermute only.
A program may use at most 64 MiB of HBM per device.

v0:
```python
import jax
import jax.numpy as jnp
from jax import lax
from jax.sharding import PartitionSpec as P

BLK = 256


def exact_dot(left, right):
    return jnp.dot(left, right, precision=lax.Precision.HIGHEST, preferred_element_type=jnp.float32)


def body(front, contrib, target, mask, panel, pivots):
    row_count = lax.axis_size("row")
    col_count = lax.axis_size("col")
    row_index = lax.axis_index("row")
    col_index = lax.axis_index("col")
    tile_rows, tile_cols = front.shape
    blocks_own = tile_rows // BLK
    sent_count = contrib.shape[0] // BLK
    targets = target.reshape(row_count, sent_count)
    own_targets = lax.dynamic_slice_in_dim(targets, row_index, 1, 0)[0]
    device_ids = jnp.arange(row_count, dtype=jnp.int32)
    chooser = (own_targets[None, :] // blocks_own == device_ids[:, None]).astype(jnp.bfloat16)
    pieces = contrib.reshape(sent_count, BLK, tile_cols)
    outgoing = jnp.einsum(
        "db,bxc->dxc", chooser, pieces, preferred_element_type=jnp.float32
    ).astype(jnp.bfloat16)
    arrived = lax.all_to_all(outgoing, "row", split_axis=0, concat_axis=0, tiled=True)
    source_targets = jnp.take(targets, device_ids, axis=0)
    block_ids = jnp.arange(blocks_own, dtype=jnp.int32)
    own_blocks = row_index * blocks_own + block_ids
    placing = jnp.sum(
        (source_targets[:, :, None] == own_blocks[None, None, :]).astype(jnp.float32), axis=1
    ).astype(jnp.bfloat16)
    added = jnp.einsum("sk,sxc->kxc", placing, arrived, preferred_element_type=jnp.float32).reshape(
        tile_rows, tile_cols
    )
    assembled = front + added
    panel_rows = panel.shape[0]
    panel_start = (row_index * col_count + col_index) * panel_rows
    select_rows = (
        pivots[:, None] - panel_start == jnp.arange(panel_rows, dtype=jnp.int32)[None, :]
    ).astype(jnp.float32)
    pivot_block = lax.psum(exact_dot(select_rows, panel), ("row", "col"))
    gram = exact_dot(pivot_block, pivot_block.T)
    factor_low = jnp.linalg.cholesky(gram)
    inverse = jax.scipy.linalg.cho_solve((factor_low, True), pivot_block).T
    local_start = row_index * tile_rows
    picker = (
        pivots[:, None] - local_start == jnp.arange(tile_rows, dtype=jnp.int32)[None, :]
    ).astype(jnp.float32)
    upper = lax.psum(exact_dot(picker, assembled), "row")
    lower_own = exact_dot(panel, inverse)
    update = exact_dot(lax.all_gather(lower_own, "col", axis=0, tiled=True), upper)
    row_mask = jnp.repeat(mask[:, 0].astype(jnp.float32), BLK)
    schur = assembled - row_mask[:, None] * update
    return (lower_own, schur)


def solution(mesh):
    placed = (P("row", "col"), P("row", "col"), P(), P("row", "col"), P(("row", "col"), None), P())
    return jax.shard_map(
        body,
        mesh=mesh,
        in_specs=placed,
        out_specs=(P(("row", "col"), None), P("row", "col")),
        check_vma=False,
    )
```

profile of v0, /device:TPU:2, one launch (start us, length us, event | category | flops | bytes accessed | tf_op | source)
XLA Modules:
  0.0 1228.4 jit_solution(2532103232973570547)
XLA Ops:
  8.0 0.9 reshape.68
  8.9 0.7 copy-done
  9.6 1.8 convolution_convert_fusion
  11.4 4.7 copy.22
  16.1 12.4 %all-to-all-start = ((bf16[64,256,128]{2,1,0:T(8,128)(2,1)}), bf16[64,256,128]{2,1,0:T(8,128)(2,1)}, u32[]{:S(2)}, u32[]{:S(2)}) async-start(bf16[64,256,128]{2,1,0:T(8,128)(2,1)} %copy.22), calls=%async_computation | async-start | bytes 8388608 | tf_op jit(solution)/shard_map/all_to_all | solution.py:29
  28.5 0.0 all-reduce.4.cloned.1.call-start
  28.6 1.0 fusion.12
  29.6 0.0 all-reduce.4.cloned.1.call-update
  29.7 0.2 all-gather.2.cloned.1.call-start
  29.9 474.1 %all-reduce.4.cloned.1.call-done = f32[256,256]{1,0:T(8,128)} async-done(((f32[256,256]{1,0:T(8,128)}), f32[256,256]{1,0:T(8,128)}) %all-reduce.4.cloned.1.call-update) | async-done | bytes 262160 | tf_op jit(solution)/shard_map/psum | solution.py:45
  504.0 1.5 fusion.30
  505.5 0.1 copy.19
  505.7 11.7 cholesky.50
  517.5 9.8 custom-call.18
  527.3 0.2 constant_dynamic-update-slice_fusion
  527.5 0.3 convolution_subtract_fusion.2
  527.7 11.7 cholesky.105
  539.5 0.7 compare_reduce_fusion
  541.6 0.1 triangular_solve.66
  541.6 4.2 while.1
  541.8 0.6 fusion.46
  542.4 1.4 bitcast_dynamic-update-slice_fusion.2
  543.9 0.6 fusion.46
  544.5 1.4 bitcast_dynamic-update-slice_fusion.2
  545.9 0.6 copy-done.6
  546.5 20.5 %custom-call.19 = f32[2,128,128]{1,2,0:T(8,128)S(1)} custom-call(f32[2,128,128]{2,1,0:T(8,128)} %copy-done.6), custom_call_target="InvertDiagBlocksLowerTriangular" | custom-call | tf_op jit(solution)/shard_map/jit(_cho_solve)/triangular_solve | solution.py:48
  567.0 0.3 fusion.10
  567.4 0.3 convolution_subtract_fusion.1
  567.6 0.3 fusion.19
  568.0 0.3 fusion.18
  568.2 0.3 convolution_subtract_fusion
  568.5 0.3 fusion.17
  568.8 1.0 convolution_bitcast_fusion
  569.8 0.0 all-gather.2.cloned.1.call-update
  569.9 0.0 all-reduce.6.cloned.1.call-start
  569.9 0.6 gather_fusion
  570.6 0.1 broadcast_select_fusion
  570.6 0.1 copy.20
  570.7 0.1 convert_reduce_fusion
  570.8 4.5 fusion
  575.4 0.1 bitcast_add_fusion
  575.5 1.3 fusion.4
  576.8 0.0 all-reduce.6.cloned.1.call-update
  576.9 0.1 broadcast_bitcast_fusion
  576.9 0.8 copy.25
  577.7 41.3 %all-gather.2.cloned.1.call-done = f32[1024,256]{0,1:T(8,128)} async-done(((f32[128,256]{0,1:T(8,128)}), f32[1024,256]{0,1:T(8,128)}) %all-gather.2.cloned.1.call-update) | async-done | bytes 1048592 | tf_op jit(solution)/shard_map/all_gather | solution.py:55
  619.0 598.1 %all-reduce.6.cloned.1.call-done = f32[256,128]{1,0:T(8,128)} async-done(((f32[256,128]{1,0:T(8,128)}), f32[256,128]{1,0:T(8,128)}) %all-reduce.6.cloned.1.call-update) | async-done | bytes 131088 | tf_op jit(solution)/shard_map/psum | solution.py:53
  1217.1 3.9 fusion.3
  (34 shorter events, 0.3 us)
Async XLA Ops:
  8.0 1.6 copy-start
  16.1 12.5 %copy-start.5 = (s32[256]{0:T(256)S(1)}, s32[256]{0:T(256)}, u32[]{:S(2)}) copy-start(s32[256]{0:T(256)} %param.11) | copy-start | bytes 3076
  16.1 12.5 %copy-start.4 = (f32[128,256]{1,0:T(8,128)S(1)}, f32[128,256]{1,0:T(8,128)}, u32[]{:S(2)}) copy-start(f32[128,256]{1,0:T(8,128)} %param.10) | copy-start | bytes 393220
  16.1 554.7 %all-to-all-start = ((bf16[64,256,128]{2,1,0:T(8,128)(2,1)}), bf16[64,256,128]{2,1,0:T(8,128)(2,1)}, u32[]{:S(2)}, u32[]{:S(2)}) async-start(bf16[64,256,128]{2,1,0:T(8,128)(2,1)} %copy.22), calls=%async_computation | async-start | bytes 8388608 | tf_op jit(solution)/shard_map/all_to_all | solution.py:29
  28.5 475.4 %all-reduce.4.cloned.1.call-start = ((), (), s32[]{:S(2)}) async-start(), calls=%async_computation.1 | async-start | bytes 524288 | tf_op jit(solution)/shard_map/psum | solution.py:45
  29.6 541.2 %copy-start.7 = (s32[4,1]{0,1:T(1,128)S(1)}, s32[4,1]{0,1:T(1,128)}, u32[]{:S(2)}) copy-start(s32[4,1]{0,1:T(1,128)} %param.9) | copy-start | bytes 52
  29.7 589.3 %all-gather.2.cloned.1.call-start = ((), (), s32[]{:S(2)}) async-start(), calls=%async_computation.2 | async-start | bytes 1179648 | tf_op jit(solution)/shard_map/all_gather | solution.py:55
  504.0 63.1 %copy-start.1 = (f32[256,256]{1,0:T(8,128)S(1)}, f32[256,256]{1,0:T(8,128)}, u32[]{:S(2)}) copy-start(f32[256,256]{1,0:T(8,128)} %all-reduce.4.cloned.1.call-done) | copy-start | bytes 786436
  545.9 0.7 copy-start.6
  567.6 7.8 copy-start.3
  569.9 647.2 %all-reduce.6.cloned.1.call-start = ((), (), s32[]{:S(2)}) async-start(), calls=%async_computation.3 | async-start | bytes 262144 | tf_op jit(solution)/shard_map/psum | solution.py:53
  570.5 6.4 copy-start.2
Sparse Core Ops, SparseCore 0:
  35.4 468.5 all-reduce.3
  570.0 48.9 all-gather.1
Sparse Core Ops, SparseCore 1:
  576.9 640.1 all-reduce.5
where the time goes:
time: 1230 us
  waiting for transfers between devices  1110 us (90%)
  other arithmetic  54.8 us (4%)
  matrix products  17.3 us (1%)
  between operations  17.1 us (1%)
  local copies, waits for them, and re-layouts  12.7 us (1%)
  starting transfers between devices  12.7 us (1%)
    psum x1, waiting for transfers between devices, body(): upper = lax.psum(exact_dot(picker, assembled), 'row')  598 us
    psum x1, waiting for transfers between devices, body(): pivot_block = lax.psum(exact_dot(select_rows, panel), ('row', 'col'))  474 us
    all_gather x1, waiting for transfers between devices, body(): lax.all_gather(lower_own, 'col', axis=0, tiled=True)  41.3 us
    another operation x6, other arithmetic, body(): factor_low = jnp.linalg.cholesky(gram)  34 us
  transfers between devices with their start and end apart: 4, of which 3 were waited for; matrix products, arithmetic and copies ran while one was open for 6% of the time, Pallas kernels for 0%

commit v1 on v0

--- a/solution.py
+++ b/solution.py
@@ -2,6 +2,7 @@
 import jax.numpy as jnp
 from jax import lax
 from jax.sharding import PartitionSpec as P
+from jax.lax import psum
 
 BLK = 256
 
@@ -42,7 +43,9 @@
     select_rows = (
         pivots[:, None] - panel_start == jnp.arange(panel_rows, dtype=jnp.int32)[None, :]
     ).astype(jnp.float32)
-    pivot_block = lax.psum(exact_dot(select_rows, panel), ("row", "col"))
+    pivot_block = exact_dot(select_rows, panel)
+    for dd in ("row", "col"):
+        pivot_block = psum(pivot_block, dd)
     gram = exact_dot(pivot_block, pivot_block.T)
     factor_low = jnp.linalg.cholesky(gram)
     inverse = jax.scipy.linalg.cho_solve((factor_low, True), pivot_block).T

time: 1230 us -> 1050 us (0.85)
  the two profiles are of different devices: /device:TPU:2 before, /device:TPU:97 now
where the time goes in v1:
time: 1050 us
  waiting for transfers between devices  934 us (89%)
  other arithmetic  54.8 us (5%)
  matrix products  19 us (2%)
  between operations  15.3 us (1%)
  local copies, waits for them, and re-layouts  14.8 us (1%)
  starting transfers between devices  11 us (1%)
    psum x2, waiting for transfers between devices, body(): pivot_block = psum(pivot_block, dd)  793 us
    all_to_all x1, waiting for transfers between devices, body(): lax.all_to_all(outgoing, 'row', split_axis=0, concat_axis=0, tiled=True)  89.6 us
    all_gather x1, waiting for transfers between devices, body(): lax.all_gather(lower_own, 'col', axis=0, tiled=True)  52.1 us
    another operation x6, other arithmetic, body(): factor_low = jnp.linalg.cholesky(gram)  34 us
  transfers between devices with their start and end apart: 4, of which 4 were waited for; matrix products, arithmetic and copies ran while one was open for 0% of the time, Pallas kernels for 0%

profile of v1, /device:TPU:97, one launch (start us, length us, event | category | flops | bytes accessed | tf_op | source)
XLA Modules:
  0.0 1049.5 jit_solution(17896690102860368113)
XLA Ops:
  7.2 0.9 reshape.68
  8.1 0.7 copy-done
  8.8 1.8 convolution_convert_fusion
  10.6 4.7 copy.22
  15.3 10.7 %all-to-all-start = ((bf16[64,256,128]{2,1,0:T(8,128)(2,1)}), bf16[64,256,128]{2,1,0:T(8,128)(2,1)}, u32[]{:S(2)}, u32[]{:S(2)}) async-start(bf16[64,256,128]{2,1,0:T(8,128)(2,1)} %copy.22), calls=%async_computation | async-start | bytes 8388608 | tf_op jit(solution)/shard_map/all_to_all | solution.py:30
  26.0 0.0 all-reduce.7.cloned.1.call-start
  26.1 0.6 gather_fusion
  26.7 0.1 broadcast_select_fusion
  26.8 0.1 copy.20
  26.8 0.1 convert_reduce_fusion
  27.0 1.0 fusion.12
  28.0 89.6 %all-to-all-done = bf16[64,256,128]{2,1,0:T(8,128)(2,1)} async-done(((bf16[64,256,128]{2,1,0:T(8,128)(2,1)}), bf16[64,256,128]{2,1,0:T(8,128)(2,1)}, u32[]{:S(2)}, u32[]{:S(2)}) %all-to-all-start) | async-done | bytes 4194336 | tf_op jit(solution)/shard_map/all_to_all | solution.py:30
  117.6 4.5 fusion
  122.1 0.1 bitcast_add_fusion
  122.2 1.3 fusion.4
  123.5 0.0 all-reduce.7.cloned.1.call-update
  123.6 0.0 all-reduce.5.cloned.1.call-start
  123.6 633.5 %all-reduce.7.cloned.1.call-done = (f32[256,256]{1,0:T(8,128)}, f32[256,128]{1,0:T(8,128)}) async-done(((f32[256,256]{1,0:T(8,128)}, f32[256,128]{1,0:T(8,128)}), (f32[256,256]{1,0:T(8,128)}, f32[256,128]{1,0:T(8,128)})) %all-reduce.7.cloned.1.call-update) | async-done | bytes 393232 | tf_op jit(solution)/shard_map/psum | solution.py:48
  757.1 0.0 all-reduce.5.cloned.1.call-update
  757.1 0.2 all-gather.2.cloned.1.call-start
  757.4 159.2 %all-reduce.5.cloned.1.call-done = f32[256,256]{1,0:T(8,128)} async-done(((f32[256,256]{1,0:T(8,128)}), f32[256,256]{1,0:T(8,128)}) %all-reduce.5.cloned.1.call-update) | async-done | bytes 262160 | tf_op jit(solution)/shard_map/psum | solution.py:48
  916.6 1.5 fusion.30
  918.1 0.1 copy.19
  918.3 0.7 copy-done.2
  919.0 11.7 %cholesky.50 = f32[128,128]{1,0:T(8,128)S(1)} custom-call(f32[128,128]{1,0:T(8,128)S(1)} %cholesky.118), custom_call_target="Cholesky" | custom-call | tf_op jit(solution)/shard_map/jit(cholesky)/cholesky | solution.py:50
  930.8 9.8 custom-call.18
  940.6 1.0 constant_dynamic-update-slice_fusion
  941.7 1.1 convolution_subtract_fusion.2
  942.8 11.7 %cholesky.105 = f32[128,128]{1,0:T(8,128)S(1)} custom-call(f32[128,128]{1,0:T(8,128)S(1)} %convolution_subtract_fusion.2), custom_call_target="Cholesky" | custom-call | tf_op jit(solution)/shard_map/jit(cholesky)/cholesky | solution.py:50
  954.5 0.7 compare_reduce_fusion
  956.5 0.1 triangular_solve.66
  956.6 5.4 while.1
  956.8 0.6 fusion.46
  957.4 2.0 bitcast_dynamic-update-slice_fusion.2
  959.4 0.6 fusion.46
  960.0 2.0 bitcast_dynamic-update-slice_fusion.2
  962.0 20.5 %custom-call.19 = f32[2,128,128]{1,2,0:T(8,128)S(1)} custom-call(f32[2,128,128]{2,1,0:T(8,128)} %get-tuple-element.9), custom_call_target="InvertDiagBlocksLowerTriangular" | custom-call | tf_op jit(solution)/shard_map/jit(_cho_solve)/triangular_solve | solution.py:51
  982.5 0.3 fusion.10
  982.8 0.3 convolution_subtract_fusion.1
  983.0 0.3 fusion.19
  983.4 0.3 fusion.18
  983.6 0.3 convolution_subtract_fusion
  984.0 0.3 fusion.17
  984.2 1.0 convolution_bitcast_fusion
  985.3 0.1 broadcast_bitcast_fusion
  985.4 1.7 copy.25
  987.0 52.1 %all-gather.2.cloned.1.call-done = f32[1024,256]{0,1:T(8,128)} async-done(((f32[128,256]{0,1:T(8,128)}), f32[1024,256]{0,1:T(8,128)}) %all-gather.2.cloned.1.call-update) | async-done | bytes 1048592 | tf_op jit(solution)/shard_map/all_gather | solution.py:58
  1039.2 3.9 fusion.3
  (32 shorter events, 0.3 us)
Async XLA Ops:
  7.2 1.6 copy-start
  15.3 11.7 %copy-start.5 = (s32[256]{0:T(256)S(1)}, s32[256]{0:T(256)}, u32[]{:S(2)}) copy-start(s32[256]{0:T(256)} %param.11) | copy-start | bytes 3076
  15.3 11.7 %copy-start.4 = (f32[128,256]{1,0:T(8,128)S(1)}, f32[128,256]{1,0:T(8,128)}, u32[]{:S(2)}) copy-start(f32[128,256]{1,0:T(8,128)} %param.10) | copy-start | bytes 393220
  15.3 102.3 %all-to-all-start = ((bf16[64,256,128]{2,1,0:T(8,128)(2,1)}), bf16[64,256,128]{2,1,0:T(8,128)(2,1)}, u32[]{:S(2)}, u32[]{:S(2)}) async-start(bf16[64,256,128]{2,1,0:T(8,128)(2,1)} %copy.22), calls=%async_computation | async-start | bytes 8388608 | tf_op jit(solution)/shard_map/all_to_all | solution.py:30
  26.0 96.1 %copy-start.3 = (f32[1024,128]{1,0:T(8,128)S(1)}, f32[1024,128]{1,0:T(8,128)}, u32[]{:S(2)}) copy-start(f32[1024,128]{1,0:T(8,128)} %param.6) | copy-start | bytes 1572868
  26.0 731.1 %all-reduce.7.cloned.1.call-start = ((), (), s32[]{:S(2)}) async-start(), calls=%async_computation.3 | async-start | bytes 786432 | tf_op jit(solution)/shard_map/psum | solution.py:48
  123.5 861.7 %copy-start.6 = (s32[4,1]{0,1:T(1,128)S(1)}, s32[4,1]{0,1:T(1,128)}, u32[]{:S(2)}) copy-start(s32[4,1]{0,1:T(1,128)} %param.9) | copy-start | bytes 52
  123.6 793.0 %all-reduce.5.cloned.1.call-start = ((), (), s32[]{:S(2)}) async-start(), calls=%async_computation.1 | async-start | bytes 524288 | tf_op jit(solution)/shard_map/psum | solution.py:48
  757.1 282.0 %all-gather.2.cloned.1.call-start = ((), (), s32[]{:S(2)}) async-start(), calls=%async_computation.2 | async-start | bytes 1179648 | tf_op jit(solution)/shard_map/all_gather | solution.py:58
  916.6 65.8 %copy-start.1 = (f32[256,256]{1,0:T(8,128)S(1)}, f32[256,256]{1,0:T(8,128)}, u32[]{:S(2)}) copy-start(f32[256,256]{1,0:T(8,128)} %all-reduce.5.cloned.1.call-done) | copy-start | bytes 786436
  918.3 0.7 copy-start.2
Sparse Core Ops, SparseCore 0:
  123.7 633.3 all-reduce.6
  760.3 156.2 all-reduce.4
  985.4 53.7 all-gather.1
